TPU v7x, 32 devices: a whole 2x2x4 slice. The times are simulated.
32 devices in a mesh: groups: 2 (over x), acq: 16 (over z, y, core).
Axes of the slice: x: 2, y: 2, z: 4, core: 2. Of those that a mesh axis runs over, the one named last changes fastest.
Arguments:
- measurements: bfloat16 [128, 2, 16, 12, 256], P(('groups', 'acq')), parts along dimension 0, may hold values from -96 to 96
- tile_order: int32 [32], P('groups'), parts along dimension 0, may hold values from 0 to 15, each once
- steer_phase: float32 [32, 64, 512], P(('groups', 'acq')), parts along dimension 0, may hold values from -3.140625 to 3.140625
- group_ids: int32 [384, 256], P(('groups', 'acq')), parts along dimension 0, may hold values from 0 to 49151, as said below
Outputs:
- elevation_profile: bfloat16 [384, 256, 1024], P(('groups', 'acq')), parts along dimension 0
There are 2 independent parts, one for each index of `groups`. A program takes and returns all parts, laid end to end along the dimension named above; each array names one. Nothing has to cross between parts.
Inputs may be any that keep to these rules, and one draw needn't show every extreme that they name: `tile_order`: each tile of the window appears once. `group_ids`: equal labels mark the pixels of one joint group; the window's rows fall into bands of 3 consecutive rows (fewer at its top, and a band begins at its last row), each band's columns into runs of 3 consecutive columns (fewer at its sides; in the last band a run begins at the last column), and each band-run rectangle is one group; a group's label is the flat index row * 256 + column of its top-left pixel.
All inputs are finite; a program needn't handle non-finite values.
Results may differ from a plain program's by a relative error of at most 0.0054.
Values may be sent and summed in bfloat16 or wider, within the bound.
No kernel may reach another device: no remote copies, remote signals or barrier semaphores. Data moves between devices by JAX's collectives and lax.ppermute only.
A program may use at most 128 MiB of HBM per device.

v0:
```python
import functools
import math

import jax
import jax.numpy as jnp
from jax import lax
from jax.experimental import pallas as pl
from jax.experimental.pallas import tpu as pltpu
from jax.sharding import PartitionSpec as P


ITERS = 3
BAND = 3
STEP_SIZE = 0.0625
SHRINK_LEVEL = 3.0


def dot(a, b, dims=((1,), (0,))):
    return lax.dot_general(a, b, (dims, ((), ())), preferred_element_type=jnp.float32)


def order_kernel(order_ref, *refs, spans, ahead_rows):
    stack_ref, sent_refs = refs[0], refs[1:]
    acqs, parts, _, tiles, columns = stack_ref.shape
    lines = acqs * parts * tiles
    share = acqs * parts
    target = lax.broadcasted_iota(jnp.int32, (lines, 1), 0)
    source = lax.broadcasted_iota(jnp.int32, (1, lines), 1)
    block = lax.rem(source, tiles)
    part = lax.rem(lax.div(source, tiles), parts)
    acq = lax.div(source, tiles * parts)
    tile = jnp.zeros((1, lines), jnp.int32)
    for k in range(tiles):
        tile = jnp.where(block == k, order_ref[k], tile)
    after = jnp.where(tile == tiles - 1, 0, tile + 1)
    inner = part * acqs + acq
    pick = jnp.where(target == tile * share + inner, 1.0, 0.0).astype(jnp.bfloat16)
    pick_after = jnp.where(target == after * share + inner, 1.0, 0.0).astype(jnp.bfloat16)
    for sent_ref, span in zip(sent_refs, spans):
        for q, row in enumerate(span):
            lump = stack_ref[:, :, row].reshape(lines, columns)
            chosen = pick_after if row in ahead_rows else pick
            sent_ref[:, q * columns : (q + 1) * columns] = dot(chosen, lump).astype(sent_ref.dtype)


def order_tiles(measurements, tile_order, spans, ahead_rows):
    acqs, parts, tiles, _, columns = measurements.shape
    stack = measurements.transpose(0, 1, 3, 2, 4)
    lines = acqs * parts * tiles
    whole = pl.BlockSpec(memory_space=pltpu.VMEM)
    return pl.pallas_call(
        functools.partial(order_kernel, spans=spans, ahead_rows=ahead_rows),
        in_specs=[pl.BlockSpec(memory_space=pltpu.SMEM), whole],
        out_specs=[whole] * len(spans),
        out_shape=[
            jax.ShapeDtypeStruct((lines, len(span) * columns), measurements.dtype) for span in spans
        ],
        name="order_tiles",
    )(tile_order, stack)


def run_sums(energy, pick):
    return dot(pick, energy.astype(jnp.bfloat16))


def shrink_factor(sums, pick):
    factor = jnp.maximum(1.0 - SHRINK_LEVEL * lax.rsqrt(jnp.maximum(sums, SHRINK_LEVEL**2)), 0.0)
    high = factor.astype(jnp.bfloat16)
    low = (factor - high.astype(jnp.float32)).astype(jnp.bfloat16)
    both = jnp.concatenate([high, low], axis=0)
    return dot(jnp.concatenate([pick, pick], axis=0), both, ((0,), (0,)))


def band_kernel(active_ref, *refs, edge, apart, base, held):
    settings = dict(edge=edge, apart=apart, base=base, held=held)
    if not edge:
        return band_body(*refs, **settings)

    @pl.when(active_ref[0] > 0)
    def _():
        band_body(*refs, **settings)


def band_body(target_ref, run_ref, *refs, edge, apart, base, held):
    refs = list(refs)
    back_refs = [refs.pop(0) for _ in range(2 if edge else 1)]
    ahead_refs = [refs.pop(0) for _ in range(2 if edge else 1)]
    if held:
        refs.pop(0)
    out_ref = refs.pop(0)
    above_ref = refs.pop(0) if edge else None
    target_sc, resid_sc, step_sc, past_sc, energy_sc, factor_sc, image_sc, sem = refs
    step = pl.program_id(0)
    steps = pl.num_programs(0)
    columns = run_ref.shape[2]
    elevations = factor_sc.shape[2]
    tile_width = energy_sc.shape[2]
    groups = -(-(columns // BAND + 2) // 16) * 16
    weight_of = (0,) + (len(back_refs) - 1,) * (BAND - 1)
    set_of = (0 if apart else 1,) + (1,) * (BAND - 1)
    span = [slice(q * columns, (q + 1) * columns) for q in range(BAND)]

    def copies(of):
        first = BAND * (base + of) - 1
        targets = [above_ref if edge and q == 0 else out_ref.at[first + q] for q in range(BAND)]
        return [pltpu.make_async_copy(image_sc.at[q], targets[q], sem.at[q]) for q in range(BAND)]

    group = lax.broadcasted_iota(jnp.int32, (groups, columns), 0)
    picks = [
        jnp.where(group == run_ref[0, n : n + 1], 1.0, 0.0).astype(jnp.bfloat16)
        for n in range(run_ref.shape[1])
    ]
    target_sc[...] = target_ref[...].T

    def descend(is_first):
        for at in range(0, elevations, tile_width):
            real = slice(at, at + tile_width)
            imag = slice(elevations + at, elevations + at + tile_width)
            for q in range(BAND):
                if is_first:
                    resid = target_sc[span[q]]
                else:
                    resid = resid_sc[span[q]]
                step_real = dot(resid, back_refs[weight_of[q]][:, real])
                step_imag = dot(resid, back_refs[weight_of[q]][:, imag])
                if not is_first:
                    step_real += past_sc[span[q], real]
                    step_imag += past_sc[span[q], imag]
                step_sc[span[q], real] = step_real
                step_sc[span[q], imag] = step_imag
                energy = step_real * step_real + step_imag * step_imag
                slot = 2 * (at // tile_width) + set_of[q]
                if q > 0 and set_of[q] == set_of[q - 1]:
                    energy += energy_sc[slot]
                energy_sc[slot] = energy

        for at in range(0, elevations, tile_width):
            real = slice(at, at + tile_width)
            slot = 2 * (at // tile_width)
            sums = run_sums(energy_sc[slot + 1], picks[-1])
            if apart:
                alone = run_sums(energy_sc[slot], picks[0])
                factor_sc[0, :, real] = shrink_factor(alone, picks[0])
            factor_sc[1, :, real] = shrink_factor(sums, picks[-1])

    def predict():
        for q in range(BAND):
            guess = jnp.zeros((columns, target_sc.shape[1]), jnp.float32)
            for half in range(2):
                part = slice(half * elevations, (half + 1) * elevations)
                settled = step_sc[span[q], part] * factor_sc[set_of[q]]
                past_sc[span[q], part] = settled
                guess += dot(settled.astype(jnp.bfloat16), ahead_refs[weight_of[q]][part])
            resid_sc[span[q]] = (target_sc[span[q]].astype(jnp.float32) - guess).astype(
                jnp.bfloat16
            )

    descend(True)

    @pl.loop(1, ITERS)
    def _(i):
        predict()
        descend(False)

    @pl.when(step > 0)
    def _():
        for copy in copies(step - 1):
            copy.wait()

    for q in range(BAND):
        for half in range(2):
            part = slice(half * elevations, (half + 1) * elevations)
            image_sc[q, :, part] = (step_sc[span[q], part] * factor_sc[set_of[q]]).astype(
                image_sc.dtype
            )
        copies(step)[q].start()

    @pl.when(step == steps - 1)
    def _():
        for copy in copies(step):
            copy.wait()


def invert(active, targets, runs, backs, aheads, out_shape, *, offset, base, edge=False, apart=False, out=None):
    lines = targets.shape[0]
    steps, kinds, columns = runs.shape
    elevations = backs[0].shape[1] // 2
    whole = pl.BlockSpec(memory_space=pltpu.VMEM)
    far = pl.BlockSpec(memory_space=pl.ANY)
    pixels = BAND * columns
    tile_width = 256
    shape = jax.ShapeDtypeStruct(out_shape, jnp.bfloat16)
    above = jax.ShapeDtypeStruct(out_shape[1:], jnp.bfloat16)
    weights = [*backs, *aheads]
    extra = [] if out is None else [out]
    return pl.pallas_call(
        functools.partial(
            band_kernel, edge=edge, apart=apart, base=base, held=out is not None
        ),
        grid=(steps,),
        in_specs=[
            pl.BlockSpec(memory_space=pltpu.SMEM),
            pl.BlockSpec((lines, pixels), lambda i: (0, i + offset)),
            pl.BlockSpec((1, kinds, columns), lambda i: (i, 0, 0)),
        ]
        + [whole] * len(weights)
        + [far] * len(extra),
        out_specs=[far, far] if edge else far,
        out_shape=[shape, above] if edge else shape,
        input_output_aliases={} if out is None else {3 + len(weights): 0},
        scratch_shapes=[
            pltpu.VMEM((pixels, lines), jnp.bfloat16),
            pltpu.VMEM((pixels, lines), jnp.bfloat16),
            pltpu.VMEM((pixels, 2 * elevations), jnp.float32),
            pltpu.VMEM((pixels, 2 * elevations), jnp.float32),
            pltpu.VMEM((2 * (elevations // tile_width), columns, tile_width), jnp.float32),
            pltpu.VMEM((2, columns, elevations), jnp.float32),
            pltpu.VMEM((BAND, columns, 2 * elevations), jnp.bfloat16),
            pltpu.SemaphoreType.DMA((BAND,)),
        ],
        compiler_params=pltpu.CompilerParams(vmem_limit_bytes=40 * 1024 * 1024),
        name="invert_apart" if apart else "invert_edge" if edge else "invert",
    )(active, targets, runs, *weights, *extra)


def place_kernel(last_ref, row_ref, last_row_ref, _, out_ref, sem):
    target = out_ref.at[out_ref.shape[0] - 1]

    @pl.when(last_ref[0] > 0)
    def _():
        copy = pltpu.make_async_copy(last_row_ref, target, sem)
        copy.start()
        copy.wait()

    @pl.when(last_ref[0] == 0)
    def _():
        copy = pltpu.make_async_copy(row_ref, target, sem)
        copy.start()
        copy.wait()


def place_last_row(is_last, row, last_row, out):
    far = pl.BlockSpec(memory_space=pl.ANY)
    whole = pl.BlockSpec(memory_space=pltpu.VMEM)
    return pl.pallas_call(
        place_kernel,
        in_specs=[pl.BlockSpec(memory_space=pltpu.SMEM), whole, whole, far],
        out_specs=far,
        out_shape=jax.ShapeDtypeStruct(out.shape, out.dtype),
        input_output_aliases={3: 0},
        scratch_shapes=[pltpu.SemaphoreType.DMA],
        compiler_params=pltpu.CompilerParams(vmem_limit_bytes=4 * 1024 * 1024),
        name="place_last_row",
    )(is_last, row, last_row, out)


def turned(value, step):
    count = lax.axis_size("acq")
    return lax.ppermute(value, "acq", [(i, (i + step) % count) for i in range(count)])


def steering_of(phase):
    scale = 1.0 / math.sqrt(phase.shape[1])
    real = (jnp.cos(phase) * scale).astype(jnp.bfloat16)
    imag = (jnp.sin(phase) * scale).astype(jnp.bfloat16)
    return jnp.concatenate([real, imag], axis=1)


def planes_of(steering, acqs):
    _, lines, elevations = steering.shape
    real, imag = steering[0, : lines // 2], steering[0, lines // 2 :]
    upper = jnp.concatenate([real, -imag], axis=1).reshape(-1, 1, acqs, 2 * elevations)
    lower = jnp.concatenate([imag, real], axis=1).reshape(-1, 1, acqs, 2 * elevations)
    plane = jnp.concatenate([upper, lower], axis=1).reshape(lines, 2 * elevations)
    return plane * STEP_SIZE, plane.T


def program(measurements, tile_order, steer_phase, group_ids):
    acqs = measurements.shape[0]
    rows, columns = group_ids.shape
    elevations = steer_phase.shape[2]
    assert rows % BAND == 0
    bands = rows // BAND
    edge = [rows - 1] + list(range(BAND - 1))
    inner = [list(range(BAND * b - 1, BAND * b + 2)) for b in range(1, bands)]
    early = 1
    spans = [edge + sum(inner[:early], []), sum(inner[early:], [])]
    sent = order_tiles(measurements, tile_order, spans, (rows - 1,))
    head = lax.all_to_all(sent[0], "acq", 0, 0, tiled=True)
    tail = lax.all_to_all(sent[1], "acq", 0, 0, tiled=True)
    mine = steering_of(steer_phase)
    before = turned(mine, 1)
    back, ahead = planes_of(mine, acqs)
    back_before, ahead_before = planes_of(before, acqs)
    runs = (group_ids % columns + BAND - 1) // BAND
    first = lax.axis_index("acq") == 0
    column = jnp.arange(columns, dtype=jnp.int32)
    turn = (columns - 1) % BAND
    last_starts = jnp.maximum(0, BAND * ((column - turn + BAND) // BAND) - BAND + turn)
    last_runs = (last_starts + BAND - 1) // BAND
    apart_runs = jnp.stack([last_runs, runs[0]])[None]
    inner_runs = runs[BAND - 1 : rows - 1 : BAND][:, None]
    count = lax.axis_size("acq")
    is_first = jnp.where(first, 1, 0).reshape(1)
    is_last = jnp.where(lax.axis_index("acq") == count - 1, 1, 0).reshape(1)
    shape = (rows, columns, 2 * elevations)
    sides = dict(offset=0, base=0, edge=True)
    both = [back_before, back], [ahead_before, ahead]
    out, above = invert(is_first, head, apart_runs, *both, shape, apart=True, **sides)
    last_row = lax.ppermute(above, "acq", [(0, count - 1)])
    out = invert(
        is_first, head, inner_runs[:early], [back], [ahead], shape, offset=1, base=1, out=out
    )
    out, above = invert(1 - is_first, head, runs[:1][None], *both, shape, out=out, **sides)
    row = lax.ppermute(above, "acq", [(i, i - 1) for i in range(1, count)])
    out = invert(
        is_first, tail, inner_runs[early:], [back], [ahead], shape,
        offset=0, base=1 + early, out=out,
    )
    return place_last_row(is_last, row, last_row, out)


def solution(mesh):
    placed = (
        P(("groups", "acq"), None, None, None, None),
        P("groups"),
        P(("groups", "acq"), None, None),
        P(("groups", "acq"), None),
    )
    return jax.shard_map(
        program,
        mesh=mesh,
        in_specs=placed,
        out_specs=P(("groups", "acq"), None, None),
        check_vma=False,
    )
```

profile of v0, /device:TPU:0, one launch (start us, length us, event | category | flops | bytes accessed | tf_op | source)
XLA Modules:
  0.0 55.3 jit_solution(3815877827695123685)
XLA Ops:
  0.0 1.4 %multiply_convert_fusion.1 = (bf16[1,64,512]{2,1,0:T(8,128)(2,1)S(1)}, bf16[1,64,512]{2,1,0:T(8,128)(2,1)S(1)}) fusion(f32[1,64,512]{2,1,0:T(8,128)} %param.6), kind=kLoop, calls=%fused_computation.6 | loop fusion | flops 131072 | bytes 262144 | tf_op jit(solution)/shard_map/convert_element_type | solution.py:264
  1.4 0.5 collective-permute-start
  1.9 2.3 %order_tiles.1 = (bf16[128,1536]{1,0:T(8,128)(2,1)}, bf16[128,1536]{1,0:T(8,128)(2,1)}) custom-call(s32[16]{0:T(128)} %order_ref.1, bf16[4,2,12,16,256]{4,3,2,1,0:T(8,128)(2,1)} %bitcast.31), custom_call_target="tpu_custom_call" | custom-call | tf_op jit(solution)/shard_map/order_tiles/pallas_call | solution.py:51
  4.2 7.2 %all-to-all-start = ((bf16[16,8,1536]{2,1,0:T(8,128)(2,1)}), bf16[16,8,1536]{2,1,0:T(8,128)(2,1)S(1)}, u32[]{:S(2)}, u32[]{:S(2)}) async-start(bf16[16,8,1536]{2,1,0:T(8,128)(2,1)} %bitcast.35), calls=%async_computation | async-start | bytes 786432 | tf_op jit(solution)/shard_map/all_to_all | solution.py:289
  11.4 0.7 %add_select_fusion = s32[12,256]{1,0:T(8,128)S(1)} fusion(s32[12,256]{1,0:T(8,128)} %param.7), kind=kLoop, calls=%fused_computation.7 | loop fusion | flops 61440 | bytes 24576 | tf_op jit(solution)/shard_map/jit(floor_divide)/jit(_where)/select_n | solution.py:295
  12.3 0.1 maximum_maximum_fusion.1
  12.4 0.1 reshape.129
  12.6 0.2 copy.32
  12.8 0.0 collective-permute-done
  12.9 0.1 maximum_maximum_fusion
  13.0 0.1 reshape.128
  13.1 0.2 copy.31
  13.3 10.3 %all-to-all-done = bf16[16,8,1536]{2,1,0:T(8,128)(2,1)S(1)} async-done(((bf16[16,8,1536]{2,1,0:T(8,128)(2,1)}), bf16[16,8,1536]{2,1,0:T(8,128)(2,1)S(1)}, u32[]{:S(2)}, u32[]{:S(2)}) %all-to-all-start) | async-done | bytes 393248 | tf_op jit(solution)/shard_map/all_to_all | solution.py:289
  23.6 3.6 %all-to-all-start.1 = ((bf16[16,8,1536]{2,1,0:T(8,128)(2,1)}), bf16[16,8,1536]{2,1,0:T(8,128)(2,1)S(1)}, u32[]{:S(2)}, u32[]{:S(2)}) async-start(bf16[16,8,1536]{2,1,0:T(8,128)(2,1)} %bitcast.34), calls=%async_computation.1 | async-start | bytes 786432 | tf_op jit(solution)/shard_map/all_to_all | solution.py:290
  27.2 5.4 %invert_apart.1 = (bf16[12,256,1024]{2,1,0:T(8,128)(2,1)}, bf16[256,1024]{1,0:T(8,128)(2,1)S(1)}) custom-call(s32[1]{0:T(128)} %bitcast.1.active_ref, bf16[128,1536]{1,0:T(8,128)(2,1)S(1)} %bitcast.25, s32[1,2,256]{2,1,0:T(2,128)S(1)} %add_bitcast_fusion.refs_1_, bf16[128,1024]{1,0:T(8,128)(2,1)S(1)} %broadcast_multiply_fusion.1.refs_2_, ...), custom_call_target="tpu_custom_call" | custom-call | tf_op jit(solution)/shard_map/invert_apart/pallas_call | solution.py:196
  32.6 4.9 %invert.2.refs_6_ = bf16[12,256,1024]{2,1,0:T(8,128)(2,1)} custom-call(s32[1]{0:T(128)} %bitcast.1.active_ref, bf16[128,1536]{1,0:T(8,128)(2,1)S(1)} %bitcast.26, s32[1,1,256]{2,1,0:T(1,128)S(1)} %slice_bitcast_fusion.refs_1_, bf16[128,1024]{1,0:T(8,128)(2,1)S(1)} %broadcast_multiply_fusion.refs_3_.refs_2_, ...), custom_call_target="tpu_custom_call", output_to_operand_aliasing={{}: (5, {})} | custom-call | tf_op jit(solution)/shard_map/invert/pallas_call | solution.py:196
  37.5 1.3 %collective-permute-start.1 = (bf16[256,1024]{1,0:T(8,128)(2,1)S(1)}, bf16[256,1024]{1,0:T(8,128)(2,1)S(1)}, u32[]{:S(2)}, u32[]{:S(2)}) collective-permute-start(bf16[256,1024]{1,0:T(8,128)(2,1)S(1)} %get-tuple-element.13), channel_id=1, source_target_pairs={{1,0},{2,1},{3,2},{4,3},{5,4},{6,5},{7,6},{8,7},{9,8},{10,9},{11,1... | collective-permute-start | bytes 1572872 | tf_op jit(solution)/shard_map/ppermute | solution.py:315
  38.8 6.7 %collective-permute-start.2 = (bf16[256,1024]{1,0:T(8,128)(2,1)S(1)}, bf16[256,1024]{1,0:T(8,128)(2,1)S(1)}, u32[]{:S(2)}, u32[]{:S(2)}) collective-permute-start(bf16[256,1024]{1,0:T(8,128)(2,1)S(1)} %get-tuple-element.14), channel_id=1, source_target_pairs={{0,15},{16,31}} | collective-permute-start | bytes 1572872 | tf_op jit(solution)/shard_map/ppermute | solution.py:310
  45.6 0.0 all-to-all-done.1
  45.6 8.8 %invert.3._ = bf16[12,256,1024]{2,1,0:T(8,128)(2,1)} custom-call(s32[1]{0:T(128)} %bitcast.1.active_ref, bf16[128,1536]{1,0:T(8,128)(2,1)S(1)} %bitcast.30, s32[2,1,256]{2,1,0:T(1,128)S(1)} %slice.32.refs_1_, bf16[128,1024]{1,0:T(8,128)(2,1)S(1)} %broadcast_multiply_fusion.refs_3_.refs_2_, ...), custom_call_target="tpu_custom_call", output_to_operand_aliasing={{}: (5, {})} | custom-call | tf_op jit(solution)/shard_map/invert/pallas_call | solution.py:196
  54.5 0.0 collective-permute-done.1.row_ref
  54.5 0.0 collective-permute-done.2.last_row_ref
  54.5 0.8 %place_last_row.1 = bf16[12,256,1024]{2,1,0:T(8,128)(2,1)} custom-call(s32[1]{0:T(128)} %bitcast.last_ref, bf16[256,1024]{1,0:T(8,128)(2,1)S(1)} %collective-permute-done.1.row_ref, bf16[256,1024]{1,0:T(8,128)(2,1)S(1)} %collective-permute-done.2.last_row_ref, bf16[12,256,1024]{2,1,0:T(8,128)(2,1)} %invert.3._), custom_call_target="tpu_custom_call", output_to_operand_aliasing={{}: (3, {})} | custom-call | tf_op jit(solution)/shard_map/place_last_row/pallas_call | solution.py:245
  (17 shorter events, 0.3 us)
Async XLA Ops:
  1.4 11.4 %collective-permute-start = (bf16[1,128,512]{2,1,0:T(8,128)(2,1)S(1)}, bf16[1,128,512]{2,1,0:T(8,128)(2,1)S(1)}, u32[]{:S(2)}, u32[]{:S(2)}) collective-permute-start(bf16[1,128,512]{2,1,0:T(8,128)(2,1)S(1)} %pad_maximum_fusion), channel_id=1, source_target_pairs={{0,1},{1,2},{2,3},{3,4},{4,5},{5,6},{6,7},{7,8},{8,9},{9,10},{10,1... | collective-permute-start | bytes 393224 | tf_op jit(solution)/shard_map/ppermute | solution.py:259
  4.2 19.4 %all-to-all-start = ((bf16[16,8,1536]{2,1,0:T(8,128)(2,1)}), bf16[16,8,1536]{2,1,0:T(8,128)(2,1)S(1)}, u32[]{:S(2)}, u32[]{:S(2)}) async-start(bf16[16,8,1536]{2,1,0:T(8,128)(2,1)} %bitcast.35), calls=%async_computation | async-start | bytes 786432 | tf_op jit(solution)/shard_map/all_to_all | solution.py:289
  23.6 22.0 %all-to-all-start.1 = ((bf16[16,8,1536]{2,1,0:T(8,128)(2,1)}), bf16[16,8,1536]{2,1,0:T(8,128)(2,1)S(1)}, u32[]{:S(2)}, u32[]{:S(2)}) async-start(bf16[16,8,1536]{2,1,0:T(8,128)(2,1)} %bitcast.34), calls=%async_computation.1 | async-start | bytes 786432 | tf_op jit(solution)/shard_map/all_to_all | solution.py:290
  37.5 16.9 %collective-permute-start.1 = (bf16[256,1024]{1,0:T(8,128)(2,1)S(1)}, bf16[256,1024]{1,0:T(8,128)(2,1)S(1)}, u32[]{:S(2)}, u32[]{:S(2)}) collective-permute-start(bf16[256,1024]{1,0:T(8,128)(2,1)S(1)} %get-tuple-element.13), channel_id=1, source_target_pairs={{1,0},{2,1},{3,2},{4,3},{5,4},{6,5},{7,6},{8,7},{9,8},{10,9},{11,1... | collective-permute-start | bytes 1572872 | tf_op jit(solution)/shard_map/ppermute | solution.py:315
  38.8 15.6 %collective-permute-start.2 = (bf16[256,1024]{1,0:T(8,128)(2,1)S(1)}, bf16[256,1024]{1,0:T(8,128)(2,1)S(1)}, u32[]{:S(2)}, u32[]{:S(2)}) collective-permute-start(bf16[256,1024]{1,0:T(8,128)(2,1)S(1)} %get-tuple-element.14), channel_id=1, source_target_pairs={{0,15},{16,31}} | collective-permute-start | bytes 1572872 | tf_op jit(solution)/shard_map/ppermute | solution.py:310
where the time goes:
time: 55.7 us; the launch traced here: 55.3 us
  Pallas kernels  22.3 us (40%)
  starting transfers between devices  19.3 us (35%)
  waiting for transfers between devices  10.3 us (18%)
  other arithmetic  2.56 us (5%)
  local copies, waits for them, and re-layouts  0.6 us (1%)
    pallas_call x4, Pallas kernels, invert(): pl.pallas_call(functools.partial(band_kernel, edge=edge, apart=apart, bas...  19.2 us
    all_to_all x1, waiting for transfers between devices, program(): head = lax.all_to_all(sent[0], 'acq', 0, 0, tiled=True)  10.3 us
    all_to_all x1, starting transfers between devices, program(): head = lax.all_to_all(sent[0], 'acq', 0, 0, tiled=True)  7.21 us
    ppermute x1, starting transfers between devices, program(): last_row = lax.ppermute(above, 'acq', [(0, count - 1)])  6.74 us
    all_to_all x1, starting transfers between devices, program(): tail = lax.all_to_all(sent[1], 'acq', 0, 0, tiled=True)  3.55 us
    pallas_call x1, Pallas kernels, order_tiles(): pl.pallas_call(functools.partial(order_kernel, spans=spans, ahead_rows=ah...  2.26 us
    convert_element_type x1, other arithmetic, steering_of(): real = (jnp.cos(phase) * scale).astype(jnp.bfloat16)  1.37 us
    ppermute x1, starting transfers between devices, program(): row = lax.ppermute(above, 'acq', [(i, i - 1) for i in range(1, count)])  1.29 us
  transfers between devices with their start and end apart: 5, of which 1 were waited for; matrix products, arithmetic and copies ran while one was open for 3% of the time, Pallas kernels for 39%

commit v1 on v0

--- a/solution.py
+++ b/solution.py
@@ -55,6 +55,7 @@
         out_shape=[
             jax.ShapeDtypeStruct((lines, len(span) * columns), measurements.dtype) for span in spans
         ],
+        compiler_params=pltpu.CompilerParams(vmem_limit_bytes=8 * 1024 * 1024),
         name="order_tiles",
     )(tile_order, stack)
 
@@ -304,13 +305,13 @@
     is_first = jnp.where(first, 1, 0).reshape(1)
     is_last = jnp.where(lax.axis_index("acq") == count - 1, 1, 0).reshape(1)
     shape = (rows, columns, 2 * elevations)
+    out = invert(
+        is_first, head, inner_runs[:early], [back], [ahead], shape, offset=1, base=1
+    )
     sides = dict(offset=0, base=0, edge=True)
     both = [back_before, back], [ahead_before, ahead]
-    out, above = invert(is_first, head, apart_runs, *both, shape, apart=True, **sides)
+    out, above = invert(is_first, head, apart_runs, *both, shape, apart=True, out=out, **sides)
     last_row = lax.ppermute(above, "acq", [(0, count - 1)])
-    out = invert(
-        is_first, head, inner_runs[:early], [back], [ahead], shape, offset=1, base=1, out=out
-    )
     out, above = invert(1 - is_first, head, runs[:1][None], *both, shape, out=out, **sides)
     row = lax.ppermute(above, "acq", [(i, i - 1) for i in range(1, count)])
     out = invert(

time: 55.7 us -> 56.9 us (1.022)
  local copies, waits for them, and re-layouts: 0.6 us -> 2.38 us
  Pallas kernels: 22.3 us -> 21.6 us
    unnamed x0 -> x4, local copies, waits for them, and re-layouts: none -> 1.79 us
    pallas_call x1, Pallas kernels: 2.26 us -> 1.66 us  [order_tiles(): pl.pallas_call(functools.partial(order_kernel, spans=spans, ahead_rows=ah...]
  transfers between devices with their start and end apart: 5 -> 5, of which waited for: 1 -> 1; matrix products, arithmetic and copies ran while one was open for 3% -> 3% of each run, Pallas kernels for 39% -> 37%
where the time goes in v1:
time: 56.9 us; the launch traced here: 56.4 us
  Pallas kernels  21.6 us (38%)
  starting transfers between devices  19.3 us (34%)
  waiting for transfers between devices  10.3 us (18%)
  other arithmetic  2.54 us (4%)
  local copies, waits for them, and re-layouts  2.38 us (4%)
    pallas_call x4, Pallas kernels, invert(): pl.pallas_call(functools.partial(band_kernel, edge=edge, apart=apart, bas...  19.1 us
    all_to_all x1, waiting for transfers between devices, program(): head = lax.all_to_all(sent[0], 'acq', 0, 0, tiled=True)  10.3 us
    all_to_all x1, starting transfers between devices, program(): head = lax.all_to_all(sent[0], 'acq', 0, 0, tiled=True)  7.21 us
    ppermute x1, starting transfers between devices, program(): last_row = lax.ppermute(above, 'acq', [(0, count - 1)])  6.73 us
    all_to_all x1, starting transfers between devices, program(): tail = lax.all_to_all(sent[1], 'acq', 0, 0, tiled=True)  3.55 us
    unnamed x4, local copies, waits for them, and re-layouts  1.79 us
    pallas_call x1, Pallas kernels, order_tiles(): pl.pallas_call(functools.partial(order_kernel, spans=spans, ahead_rows=ah...  1.66 us
    convert_element_type x1, other arithmetic, steering_of(): real = (jnp.cos(phase) * scale).astype(jnp.bfloat16)  1.37 us
  transfers between devices with their start and end apart: 5, of which 1 were waited for; matrix products, arithmetic and copies ran while one was open for 3% of the time, Pallas kernels for 37%

profile of v1, /device:TPU:0, one launch (start us, length us, event | category | flops | bytes accessed | tf_op | source)
XLA Modules:
  0.0 56.4 jit_solution(16298484527135701346)
XLA Ops:
  0.0 1.4 %multiply_convert_fusion.1 = (bf16[1,64,512]{2,1,0:T(8,128)(2,1)S(1)}, bf16[1,64,512]{2,1,0:T(8,128)(2,1)S(1)}) fusion(f32[1,64,512]{2,1,0:T(8,128)} %param.6), kind=kLoop, calls=%fused_computation.6 | loop fusion | flops 131072 | bytes 262144 | tf_op jit(solution)/shard_map/convert_element_type | solution.py:265
  1.4 0.5 collective-permute-start
  1.9 0.0 copy-start
  1.9 1.1 %copy-done = bf16[4,2,16,12,256]{4,2,3,1,0:T(8,128)(2,1)S(1)} copy-done((bf16[4,2,16,12,256]{4,2,3,1,0:T(8,128)(2,1)S(1)}, bf16[4,2,16,12,256]{4,2,3,1,0:T(8,128)(2,1)}, u32[]{:S(2)}) %copy-start) | copy-done | bytes 786456
  3.1 0.0 copy-start.1
  3.1 0.7 %copy-done.1 = s32[16]{0:T(128)S(1)} copy-done((s32[16]{0:T(128)S(1)}, s32[16]{0:T(128)}, u32[]{:S(2)}) %copy-start.1) | copy-done | bytes 88
  3.7 1.7 %order_tiles.1 = (bf16[128,1536]{1,0:T(8,128)(2,1)}, bf16[128,1536]{1,0:T(8,128)(2,1)}) custom-call(s32[16]{0:T(128)S(1)} %copy-done.1, bf16[4,2,12,16,256]{4,3,2,1,0:T(8,128)(2,1)S(1)} %bitcast.31), custom_call_target="tpu_custom_call" | custom-call | tf_op jit(solution)/shard_map/order_tiles/pallas_call | solution.py:51
  5.4 7.2 %all-to-all-start = ((bf16[16,8,1536]{2,1,0:T(8,128)(2,1)}), bf16[16,8,1536]{2,1,0:T(8,128)(2,1)S(1)}, u32[]{:S(2)}, u32[]{:S(2)}) async-start(bf16[16,8,1536]{2,1,0:T(8,128)(2,1)} %bitcast.3), calls=%async_computation | async-start | bytes 786432 | tf_op jit(solution)/shard_map/all_to_all | solution.py:290
  12.6 0.7 %add_select_fusion = s32[12,256]{1,0:T(8,128)S(1)} fusion(s32[12,256]{1,0:T(8,128)} %param.7), kind=kLoop, calls=%fused_computation.7 | loop fusion | flops 61440 | bytes 24576 | tf_op jit(solution)/shard_map/jit(floor_divide)/jit(_where)/select_n | solution.py:296
  13.5 0.1 maximum_maximum_fusion.1
  13.6 0.1 reshape.129
  13.7 0.2 copy.32
  13.9 0.0 collective-permute-done
  14.1 0.1 maximum_maximum_fusion
  14.2 0.1 reshape.128
  14.3 0.2 copy.31
  14.5 10.3 %all-to-all-done = bf16[16,8,1536]{2,1,0:T(8,128)(2,1)S(1)} async-done(((bf16[16,8,1536]{2,1,0:T(8,128)(2,1)}), bf16[16,8,1536]{2,1,0:T(8,128)(2,1)S(1)}, u32[]{:S(2)}, u32[]{:S(2)}) %all-to-all-start) | async-done | bytes 393248 | tf_op jit(solution)/shard_map/all_to_all | solution.py:290
  24.8 3.6 %all-to-all-start.1 = ((bf16[16,8,1536]{2,1,0:T(8,128)(2,1)}), bf16[16,8,1536]{2,1,0:T(8,128)(2,1)S(1)}, u32[]{:S(2)}, u32[]{:S(2)}) async-start(bf16[16,8,1536]{2,1,0:T(8,128)(2,1)} %bitcast.14), calls=%async_computation.1 | async-start | bytes 786432 | tf_op jit(solution)/shard_map/all_to_all | solution.py:291
  28.4 4.9 %invert.2.refs_6_ = bf16[12,256,1024]{2,1,0:T(8,128)(2,1)} custom-call(s32[1]{0:T(128)} %bitcast.1.active_ref, bf16[128,1536]{1,0:T(8,128)(2,1)S(1)} %bitcast.25, s32[1,1,256]{2,1,0:T(1,128)S(1)} %slice_bitcast_fusion.refs_1_, bf16[128,1024]{1,0:T(8,128)(2,1)S(1)} %broadcast_multiply_fusion.refs_2_.refs_3_, bf16[1024,128]{1,0:T(8,128)(2,1)S(1)} %bitcast.21), custom_call_target="tpu_custom_call" | custom-call | tf_op jit(solution)/shard_map/invert/pallas_call | solution.py:197
  33.2 5.4 %invert_apart.1 = (bf16[12,256,1024]{2,1,0:T(8,128)(2,1)}, bf16[256,1024]{1,0:T(8,128)(2,1)S(1)}) custom-call(s32[1]{0:T(128)} %bitcast.1.active_ref, bf16[128,1536]{1,0:T(8,128)(2,1)S(1)} %bitcast.26, s32[1,2,256]{2,1,0:T(2,128)S(1)} %add_bitcast_fusion.refs_1_, ...), custom_call_target="tpu_custom_call", output_to_operand_aliasing={{0}: (7, {})} | custom-call | tf_op jit(solution)/shard_map/invert_apart/pallas_call | solution.py:197
  38.7 1.3 %collective-permute-start.1 = (bf16[256,1024]{1,0:T(8,128)(2,1)S(1)}, bf16[256,1024]{1,0:T(8,128)(2,1)S(1)}, u32[]{:S(2)}, u32[]{:S(2)}) collective-permute-start(bf16[256,1024]{1,0:T(8,128)(2,1)S(1)} %get-tuple-element.13), channel_id=1, source_target_pairs={{1,0},{2,1},{3,2},{4,3},{5,4},{6,5},{7,6},{8,7},{9,8},{10,9},{11,1... | collective-permute-start | bytes 1572872 | tf_op jit(solution)/shard_map/ppermute | solution.py:316
  40.0 6.7 %collective-permute-start.2 = (bf16[256,1024]{1,0:T(8,128)(2,1)S(1)}, bf16[256,1024]{1,0:T(8,128)(2,1)S(1)}, u32[]{:S(2)}, u32[]{:S(2)}) collective-permute-start(bf16[256,1024]{1,0:T(8,128)(2,1)S(1)} %get-tuple-element.14), channel_id=1, source_target_pairs={{0,15},{16,31}} | collective-permute-start | bytes 1572872 | tf_op jit(solution)/shard_map/ppermute | solution.py:314
  46.8 0.0 all-to-all-done.1
  46.8 8.8 %invert.3._ = bf16[12,256,1024]{2,1,0:T(8,128)(2,1)} custom-call(s32[1]{0:T(128)} %bitcast.1.active_ref, bf16[128,1536]{1,0:T(8,128)(2,1)S(1)} %bitcast.30, s32[2,1,256]{2,1,0:T(1,128)S(1)} %slice.32.refs_1_, bf16[128,1024]{1,0:T(8,128)(2,1)S(1)} %broadcast_multiply_fusion.refs_2_.refs_3_, ...), custom_call_target="tpu_custom_call", output_to_operand_aliasing={{}: (5, {})} | custom-call | tf_op jit(solution)/shard_map/invert/pallas_call | solution.py:197
  55.6 0.0 collective-permute-done.1.row_ref
  55.6 0.0 collective-permute-done.2.last_row_ref
  55.6 0.8 %place_last_row.1 = bf16[12,256,1024]{2,1,0:T(8,128)(2,1)} custom-call(s32[1]{0:T(128)} %bitcast.last_ref, bf16[256,1024]{1,0:T(8,128)(2,1)S(1)} %collective-permute-done.1.row_ref, bf16[256,1024]{1,0:T(8,128)(2,1)S(1)} %collective-permute-done.2.last_row_ref, bf16[12,256,1024]{2,1,0:T(8,128)(2,1)} %invert.3._), custom_call_target="tpu_custom_call", output_to_operand_aliasing={{}: (3, {})} | custom-call | tf_op jit(solution)/shard_map/place_last_row/pallas_call | solution.py:246
  (17 shorter events, 0.3 us)
Async XLA Ops:
  1.4 12.6 %collective-permute-start = (bf16[1,128,512]{2,1,0:T(8,128)(2,1)S(1)}, bf16[1,128,512]{2,1,0:T(8,128)(2,1)S(1)}, u32[]{:S(2)}, u32[]{:S(2)}) collective-permute-start(bf16[1,128,512]{2,1,0:T(8,128)(2,1)S(1)} %pad_maximum_fusion), channel_id=1, source_target_pairs={{0,1},{1,2},{2,3},{3,4},{4,5},{5,6},{6,7},{7,8},{8,9},{9,10},{10,1... | collective-permute-start | bytes 393224 | tf_op jit(solution)/shard_map/ppermute | solution.py:260
  1.9 1.1 %copy-start = (bf16[4,2,16,12,256]{4,2,3,1,0:T(8,128)(2,1)S(1)}, bf16[4,2,16,12,256]{4,2,3,1,0:T(8,128)(2,1)}, u32[]{:S(2)}) copy-start(bf16[4,2,16,12,256]{4,2,3,1,0:T(8,128)(2,1)} %param.4) | copy-start | bytes 2359300
  3.1 0.7 %copy-start.1 = (s32[16]{0:T(128)S(1)}, s32[16]{0:T(128)}, u32[]{:S(2)}) copy-start(s32[16]{0:T(128)} %order_ref.1) | copy-start | bytes 196
  5.4 19.4 %all-to-all-start = ((bf16[16,8,1536]{2,1,0:T(8,128)(2,1)}), bf16[16,8,1536]{2,1,0:T(8,128)(2,1)S(1)}, u32[]{:S(2)}, u32[]{:S(2)}) async-start(bf16[16,8,1536]{2,1,0:T(8,128)(2,1)} %bitcast.3), calls=%async_computation | async-start | bytes 786432 | tf_op jit(solution)/shard_map/all_to_all | solution.py:290
  24.8 22.0 %all-to-all-start.1 = ((bf16[16,8,1536]{2,1,0:T(8,128)(2,1)}), bf16[16,8,1536]{2,1,0:T(8,128)(2,1)S(1)}, u32[]{:S(2)}, u32[]{:S(2)}) async-start(bf16[16,8,1536]{2,1,0:T(8,128)(2,1)} %bitcast.14), calls=%async_computation.1 | async-start | bytes 786432 | tf_op jit(solution)/shard_map/all_to_all | solution.py:291
  38.7 16.9 %collective-permute-start.1 = (bf16[256,1024]{1,0:T(8,128)(2,1)S(1)}, bf16[256,1024]{1,0:T(8,128)(2,1)S(1)}, u32[]{:S(2)}, u32[]{:S(2)}) collective-permute-start(bf16[256,1024]{1,0:T(8,128)(2,1)S(1)} %get-tuple-element.13), channel_id=1, source_target_pairs={{1,0},{2,1},{3,2},{4,3},{5,4},{6,5},{7,6},{8,7},{9,8},{10,9},{11,1... | collective-permute-start | bytes 1572872 | tf_op jit(solution)/shard_map/ppermute | solution.py:316
  40.0 15.6 %collective-permute-start.2 = (bf16[256,1024]{1,0:T(8,128)(2,1)S(1)}, bf16[256,1024]{1,0:T(8,128)(2,1)S(1)}, u32[]{:S(2)}, u32[]{:S(2)}) collective-permute-start(bf16[256,1024]{1,0:T(8,128)(2,1)S(1)} %get-tuple-element.14), channel_id=1, source_target_pairs={{0,15},{16,31}} | collective-permute-start | bytes 1572872 | tf_op jit(solution)/shard_map/ppermute | solution.py:314
